TPU v7x, 32 devices: a whole 2x2x4 slice. The times are simulated.
32 devices in a mesh: layer: 2 (over x), row: 4 (over z), col: 4 (over y, core).
Axes of the slice: x: 2, y: 2, z: 4, core: 2. Of those that a mesh axis runs over, the one named last changes fastest.
Arguments:
- covariance: float32 [16384, 8192], P(('layer', 'row'), 'col'), parts along dimension 0, may hold values from -2 to 20, as said below
- weight: bfloat16 [16384, 2, 1024], P(('layer', 'col', 'row')), parts along dimension 0, may hold values from -6 to 6
- factor_a: bfloat16 [16384, 2, 256], P(('layer', 'col', 'row')), parts along dimension 0, may hold values from -1.5 to 1.5
- factor_b: bfloat16 [4, 256, 1024], P('layer', ('row', 'col')), parts along dimension 0, may hold values from -1.5 to 1.5
Outputs:
- new_a: float32 [16384, 2, 256], P(('layer', 'col', 'row')), parts along dimension 0
- new_b: float32 [4, 256, 1024], P('layer', ('row', 'col')), parts along dimension 0
There are 2 independent parts, one for each index of `layer`. A program takes and returns all parts, laid end to end along the dimension named above; each array names one. Nothing has to cross between parts.
Inputs may be any that keep to these rules, and one draw needn't show every extreme that they name: covariance is symmetric and positive definite.
All inputs are finite; a program needn't handle non-finite values.
Results may differ from a plain program's by a relative error of at most 0.0012.
Values may be sent and summed in bfloat16 or wider, within the bound.
No kernel may reach another device: no remote copies, remote signals or barrier semaphores. Data moves between devices by JAX's collectives and lax.ppermute only.
A program may use at most 64 MiB of HBM per device.

v0:
```python
import jax
import jax.numpy as jnp
from jax import lax
from jax.sharding import PartitionSpec as P

D = 8192
O = 1024
R = 256


def reorder_slots(spread):
    side = lax.axis_size("row")
    total = side * side
    return spread.reshape(side, side, -1).transpose(1, 0, 2).reshape(total, -1)


def transpose_full(values):
    side = lax.axis_size("row")
    flat = values.reshape(side * side, -1)
    spread = lax.all_to_all(flat, ("row", "col"), split_axis=0, concat_axis=0, tiled=True)
    landed = lax.all_to_all(
        reorder_slots(spread), ("row", "col"), split_axis=0, concat_axis=0, tiled=True
    )
    return landed.reshape(values.shape)


def per_device(covariance, weight, factor_a, factor_b):
    highest = lax.Precision.HIGHEST
    row_count = weight.shape[0]
    full_b = lax.all_gather(factor_b, ("row", "col"), axis=1, tiled=True)
    right_f = full_b.astype(jnp.float32)
    diff_one = (
        weight.astype(jnp.float32)
        - jnp.einsum("nkr,kro->nko", factor_a, full_b, preferred_element_type=jnp.float32)
    ).astype(jnp.bfloat16)
    panels = lax.all_gather(
        jnp.einsum("nko,kro->nkr", diff_one, full_b, preferred_element_type=jnp.float32),
        "row",
        axis=0,
        tiled=True,
    )
    panel_flat = panels.reshape(panels.shape[0], -1)
    cov_rows = covariance
    grad_one = lax.psum_scatter(
        jnp.dot(cov_rows, panel_flat, precision=highest, preferred_element_type=jnp.float32),
        "col",
        scatter_dimension=0,
        tiled=True,
    )
    grad_one = transpose_full(grad_one)
    new_a = factor_a.astype(jnp.float32) + 4.0 / O * grad_one.reshape(row_count, 2, R)
    diff_two = (
        weight.astype(jnp.float32) - jnp.einsum("nkr,kro->nko", new_a, right_f, precision=highest)
    ).astype(jnp.bfloat16)
    a_panel = lax.all_gather(new_a.reshape(row_count, 2 * R), "row", axis=0, tiled=True)
    cov_rows = covariance
    field = lax.psum_scatter(
        jnp.dot(cov_rows, a_panel, precision=highest, preferred_element_type=jnp.float32),
        "col",
        scatter_dimension=0,
        tiled=True,
    )
    field = transpose_full(field)
    partial_value = jnp.einsum(
        "nkr,nko->kro",
        field.reshape(row_count, 2, R),
        diff_two.astype(jnp.float32),
        precision=highest,
    )
    summed = lax.psum(partial_value, ("row", "col"))
    share_rows = factor_b.shape[1]
    linear_id = lax.axis_index("row") * lax.axis_size("col") + lax.axis_index("col")
    own_share = lax.dynamic_slice_in_dim(summed, linear_id * share_rows, share_rows, 1)
    new_b = factor_b.astype(jnp.float32) + 8.0 / D * own_share
    return (new_a, new_b)


def solution(mesh):
    in_specs = (
        P(("layer", "row"), "col"),
        P(("layer", "col", "row"), None, None),
        P(("layer", "col", "row"), None, None),
        P("layer", ("row", "col"), None),
    )
    out_specs = (P(("layer", "col", "row"), None, None), P("layer", ("row", "col"), None))
    return jax.shard_map(
        per_device, mesh=mesh, in_specs=in_specs, out_specs=out_specs, check_vma=False
    )
```

profile of v0, /device:TPU:0, one launch (start us, length us, event | category | flops | bytes accessed | tf_op | source)
XLA Modules:
  0.0 676.0 jit_solution(4953905984134823521)
XLA Ops:
  7.2 0.0 copy-start.2
  7.2 0.0 all-gather.4.cloned.1.call-start
  7.2 0.7 all-gather.4.cloned.1.call-update
  7.9 0.0 all-gather.6.cloned.1.call-start
  8.0 4.7 copy.27
  12.7 38.1 %all-gather.4.cloned.1.call-done = bf16[2,256,1024]{2,1,0:T(8,128)(2,1)} async-done(((bf16[2,16,1024]{2,1,0:T(8,128)(2,1)}), bf16[2,256,1024]{2,1,0:T(8,128)(2,1)}) %all-gather.4.cloned.1.call-update) | async-done | bytes 1048592 | tf_op jit(solution)/shard_map/all_gather | solution.py:30
  50.8 0.0 copy-done.2
  50.8 4.3 fusion.3
  55.1 0.0 all-gather.6.cloned.1.call-update
  55.2 0.0 reduce-scatter.3.cloned.1.call-start
  55.2 79.8 %all-gather.6.cloned.1.call-done = f32[2048,2,256]{2,0,1:T(8,128)} async-done(((f32[512,2,256]{2,0,1:T(8,128)}), f32[2048,2,256]{2,0,1:T(8,128)}) %all-gather.6.cloned.1.call-update) | async-done | bytes 4194320 | tf_op jit(solution)/shard_map/all_gather | solution.py:36
  135.0 5.4 copy.30
  140.4 32.4 %convolution_bitcast_fusion.1 = f32[2048,512]{0,1:T(8,128)} fusion(f32[2048,512]{0,1:T(8,128)} %bitcast.35, f32[2048,2048]{1,0:T(8,128)} %param.4), kind=kOutput, calls=%fused_computation.5 | convolution fusion | flops 25769803776 | bytes 25165824 | tf_op jit(solution)/shard_map/dot_general | solution.py:45
  172.7 0.0 reduce-scatter.3.cloned.1.call-update
  172.8 0.0 all-gather.8.cloned.1.call-start
  172.8 43.0 %reduce-scatter.3.cloned.1.call-done = f32[512,512]{0,1:T(8,128)} async-done(((f32[2048,512]{0,1:T(8,128)}), f32[512,512]{0,1:T(8,128)}) %reduce-scatter.3.cloned.1.call-update) | async-done | bytes 1048592 | tf_op jit(solution)/shard_map/reduce_scatter | solution.py:44
  215.8 1.6 copy.31
  217.4 2.2 all_to_all.32
  219.6 29.9 %all_to_all.40 = f32[16,1,16384]{2,1,0:T(1,128)S(1)} all-to-all(f32[16,1,16384]{2,1,0:T(1,128)} %all_to_all.32), channel_id=1, replica_groups=mesh['layer'=2,'row'=4,'col'=4] {'row','col'}, dimensions={0} | all-to-all | bytes 2097152 | tf_op jit(solution)/shard_map/all_to_all | solution.py:20
  249.5 3.7 reduce
  253.3 1.5 reshape.39
  254.8 1.6 copy.33
  256.5 2.6 all_to_all.33
  259.1 29.5 %all_to_all.41 = f32[16,1,16384]{2,1,0:T(1,128)S(1)} all-to-all(f32[16,1,16384]{2,1,0:T(1,128)S(1)} %all_to_all.33), channel_id=1, replica_groups=mesh['layer'=2,'row'=4,'col'=4] {'row','col'}, dimensions={0} | all-to-all | bytes 2097152 | tf_op jit(solution)/shard_map/all_to_all | solution.py:21
  288.6 3.0 multiply_reduce_fusion
  291.6 1.9 mul.23
  293.4 1.5 convert_add_fusion
  294.9 0.0 copy-start
  294.9 1.1 copy.48
  296.1 0.0 all-gather.8.cloned.1.call-update
  296.1 0.0 reduce-scatter.5.cloned.1.call-start
  296.1 81.2 %all-gather.8.cloned.1.call-done = f32[2048,512]{1,0:T(8,128)} async-done(((f32[512,512]{1,0:T(8,128)}), f32[2048,512]{1,0:T(8,128)}) %all-gather.8.cloned.1.call-update) | async-done | bytes 4194320 | tf_op jit(solution)/shard_map/all_gather | solution.py:55
  377.3 57.6 %convolution_bitcast_fusion = f32[2048,512]{0,1:T(8,128)} fusion(f32[2048,512]{1,0:T(8,128)} %all-gather.8.cloned.1.call-done, f32[2048,2048]{1,0:T(8,128)} %param.4), kind=kOutput, calls=%fused_computation.4 | convolution fusion | flops 25769803776 | bytes 25165824 | tf_op jit(solution)/shard_map/dot_general | solution.py:58
  434.9 0.0 reduce-scatter.5.cloned.1.call-update
  435.0 43.1 %reduce-scatter.5.cloned.1.call-done = f32[512,512]{0,1:T(8,128)} async-done(((f32[2048,512]{0,1:T(8,128)}), f32[512,512]{0,1:T(8,128)}) %reduce-scatter.5.cloned.1.call-update) | async-done | bytes 1048592 | tf_op jit(solution)/shard_map/reduce_scatter | solution.py:57
  478.0 2.6 copy.35
  480.6 3.4 all_to_all.34
  484.0 29.5 %all_to_all.42 = f32[16,1,16384]{2,1,0:T(1,128)} all-to-all(f32[16,1,16384]{2,1,0:T(1,128)} %all_to_all.34), channel_id=1, replica_groups=mesh['layer'=2,'row'=4,'col'=4] {'row','col'}, dimensions={0} | all-to-all | bytes 2097152 | tf_op jit(solution)/shard_map/all_to_all | solution.py:20
  513.5 4.7 reduce.2
  518.3 2.5 reshape.41
  520.8 2.9 copy.57
  523.7 3.3 all_to_all.35
  527.0 5.1 all-to-all-start.3
  532.1 0.3 all-reduce.2.cloned.1.call-start
  532.4 0.0 copy-done
  532.4 4.5 fusion.1
  536.9 0.0 copy-start.1
  536.9 18.1 %all-to-all-done.3 = f32[16,1,16384]{2,1,0:T(1,128)} async-done(((f32[16,1,16384]{2,1,0:T(1,128)}), f32[16,1,16384]{2,1,0:T(1,128)}, u32[]{:S(2)}, u32[]{:S(2)}) %all-to-all-start.3) | async-done | bytes 1048608 | tf_op jit(solution)/shard_map/all_to_all | solution.py:21
  555.0 4.7 reduce.3
  559.8 2.1 reshape_reshape.4
  561.9 0.0 copy-done.1
  561.9 0.0 copy-start.3
  561.9 4.8 fusion.4
  566.7 0.0 all-reduce.2.cloned.1.call-update
  566.7 100.4 %all-reduce.2.cloned.1.call-done = f32[2,256,1024]{2,1,0:T(8,128)} async-done(((f32[2,256,1024]{2,1,0:T(8,128)}), f32[2,256,1024]{2,1,0:T(8,128)}) %all-reduce.2.cloned.1.call-update) | async-done | bytes 2097168 | tf_op jit(solution)/shard_map/psum | solution.py:70
  667.1 0.0 copy-done.3
  667.1 1.6 multiply_add_fusion
Async XLA Ops:
  7.2 43.6 %copy-start.2 = (bf16[512,2,256]{2,1,0:T(2,128)(2,1)S(1)}, bf16[512,2,256]{2,1,0:T(2,128)(2,1)}, u32[]{:S(2)}) copy-start(bf16[512,2,256]{2,1,0:T(2,128)(2,1)} %param.6) | copy-start | bytes 1572868
  7.2 43.6 %all-gather.4.cloned.1.call-start = ((), (), s32[]{:S(2)}) async-start(), calls=%async_computation.6 | async-start | bytes 1114112 | tf_op jit(solution)/shard_map/all_gather | solution.py:30
  7.9 127.1 %all-gather.6.cloned.1.call-start = ((), (), s32[]{:S(2)}) async-start(), calls=%async_computation.7 | async-start | bytes 5242880 | tf_op jit(solution)/shard_map/all_gather | solution.py:36
  55.2 160.7 %reduce-scatter.3.cloned.1.call-start = ((), (), s32[]{:S(2)}) async-start(), calls=%async_computation.8 | async-start | bytes 5242880 | tf_op jit(solution)/shard_map/reduce_scatter | solution.py:44
  172.8 204.5 %all-gather.8.cloned.1.call-start = ((), (), s32[]{:S(2)}) async-start(), calls=%async_computation.9 | async-start | bytes 5242880 | tf_op jit(solution)/shard_map/all_gather | solution.py:55
  294.9 237.5 %copy-start = (f32[128,8,256]{2,1,0:T(8,128)}, f32[128,8,256]{2,1,0:T(8,128)S(1)}, u32[]{:S(2)}) copy-start(f32[128,8,256]{2,1,0:T(8,128)S(1)} %convert_add_fusion) | copy-start | bytes 3145732
  296.1 181.9 %reduce-scatter.5.cloned.1.call-start = ((), (), s32[]{:S(2)}) async-start(), calls=%async_computation.10 | async-start | bytes 5242880 | tf_op jit(solution)/shard_map/reduce_scatter | solution.py:57
  527.0 28.0 %all-to-all-start.3 = ((f32[16,1,16384]{2,1,0:T(1,128)}), f32[16,1,16384]{2,1,0:T(1,128)}, u32[]{:S(2)}, u32[]{:S(2)}) async-start(f32[16,1,16384]{2,1,0:T(1,128)} %all_to_all.35), calls=%async_computation.5 | async-start | bytes 2097152 | tf_op jit(solution)/shard_map/all_to_all | solution.py:21
  532.1 135.0 %all-reduce.2.cloned.1.call-start = ((), (), s32[]{:S(2)}) async-start(), calls=%async_computation.11 | async-start | bytes 4194304 | tf_op jit(solution)/shard_map/psum | solution.py:70
  536.9 24.9 %copy-start.1 = (bf16[512,2,1024]{0,2,1:T(8,128)(2,1)S(1)}, bf16[512,2,1024]{0,2,1:T(8,128)(2,1)}, u32[]{:S(2)}) copy-start(bf16[512,2,1024]{0,2,1:T(8,128)(2,1)} %fusion.1) | copy-start | bytes 6291460
  561.9 105.2 %copy-start.3 = (bf16[2,16,1024]{2,1,0:T(8,128)(2,1)S(1)}, bf16[2,16,1024]{2,1,0:T(8,128)(2,1)}, u32[]{:S(2)}) copy-start(bf16[2,16,1024]{2,1,0:T(8,128)(2,1)} %param.7) | copy-start | bytes 196612
Sparse Core Ops, SparseCore 0:
  10.2 40.5 all-gather.3
  55.3 79.7 all-gather.5
  172.9 42.9 reduce-scatter.2
  296.2 81.0 all-gather.7
  435.1 42.9 reduce-scatter.4
  566.8 100.2 all-reduce.1
where the time goes:
time: 683 us; the launch traced here: 676 us
  waiting for transfers between devices  404 us (59%)
  matrix products  104 us (15%)
  blocking collectives  88.9 us (13%)
  local copies, waits for them, and re-layouts  39.6 us (6%)
  other arithmetic  19.2 us (3%)
  between operations  14.7 us (2%)
    psum x1, waiting for transfers between devices, per_device(): summed = lax.psum(partial_value, ('row', 'col'))  100 us
    all_gather x1, waiting for transfers between devices, per_device(): lax.all_gather(new_a.reshape(row_count, 2 * R), 'row', axis=0, tiled=True)  81.2 us
    all_gather x1, waiting for transfers between devices, per_device(): lax.all_gather(jnp.einsum('nko,kro->nkr', diff_one, full_b, preferred_ele...  79.8 us
    all_to_all x2, blocking collectives, transpose_full(): lax.all_to_all(flat, ('row', 'col'), split_axis=0, concat_axis=0, tiled=T...  59.4 us
    dot_general x1, matrix products, per_device(): jnp.dot(cov_rows, a_panel, precision=highest, preferred_element_type=jnp....  57.6 us
    reduce_scatter x1, waiting for transfers between devices, per_device(): lax.psum_scatter(jnp.dot(cov_rows, a_panel, precision=highest, preferred_...  43.1 us
    reduce_scatter x1, waiting for transfers between devices, per_device(): lax.psum_scatter(jnp.dot(cov_rows, panel_flat, precision=highest, preferr...  43 us
    all_gather x1, waiting for transfers between devices, per_device(): full_b = lax.all_gather(factor_b, ('row', 'col'), axis=1, tiled=True)  38.1 us
  transfers between devices with their start and end apart: 7, of which 7 were waited for; matrix products, arithmetic and copies ran while one was open for 1% of the time, Pallas kernels for 0%

commit v1 on v0

--- a/solution.py
+++ b/solution.py
@@ -52,7 +52,15 @@
     diff_two = (
         weight.astype(jnp.float32) - jnp.einsum("nkr,kro->nko", new_a, right_f, precision=highest)
     ).astype(jnp.bfloat16)
-    a_panel = lax.all_gather(new_a.reshape(row_count, 2 * R), "row", axis=0, tiled=True)
+    x = new_a.reshape(row_count, 2 * R)
+    ways, here, lap = (lax.axis_size("row"), lax.axis_index("row"), x.shape[0])
+    line, have = (x, 1)
+    while have < ways:
+        line = jnp.concatenate(
+            [line, lax.ppermute(line, "row", [(d, (d - have) % ways) for d in range(ways)])], axis=0
+        )
+        have = 2 * have
+    a_panel = jnp.roll(line, here * lap, axis=0)
     cov_rows = covariance
     field = lax.psum_scatter(
         jnp.dot(cov_rows, a_panel, precision=highest, preferred_element_type=jnp.float32),

time: 683 us -> 713 us (1.044)
  waiting for transfers between devices: 404 us -> 440 us
    ppermute x0 -> x2, waiting for transfers between devices: none -> 116 us  [per_device(): lax.ppermute(line, 'row', [(d, (d - have) % ways) for d in range(ways)])]
    all_gather x1 -> x0, waiting for transfers between devices: 81.2 us -> none  [per_device(): lax.all_gather(new_a.reshape(row_count, 2 * R), 'row', axis=0, tiled=True)]
  transfers between devices with their start and end apart: 7 -> 8, of which waited for: 7 -> 8; matrix products, arithmetic and copies ran while one was open for 1% -> 1% of each run, Pallas kernels for 0% -> 0%
where the time goes in v1:
time: 713 us; the launch traced here: 706 us
  waiting for transfers between devices  440 us (62%)
  matrix products  104 us (15%)
  blocking collectives  88.1 us (12%)
  local copies, waits for them, and re-layouts  33.9 us (5%)
  other arithmetic  17.2 us (2%)
  between operations  14.2 us (2%)
  starting transfers between devices  9.44 us (1%)
    ppermute x2, waiting for transfers between devices, per_device(): lax.ppermute(line, 'row', [(d, (d - have) % ways) for d in range(ways)])  116 us
    psum x1, waiting for transfers between devices, per_device(): summed = lax.psum(partial_value, ('row', 'col'))  100 us
    all_gather x1, waiting for transfers between devices, per_device(): lax.all_gather(jnp.einsum('nko,kro->nkr', diff_one, full_b, preferred_ele...  79.8 us
    all_to_all x2, blocking collectives, transpose_full(): lax.all_to_all(flat, ('row', 'col'), split_axis=0, concat_axis=0, tiled=T...  58.6 us
    dot_general x1, matrix products, per_device(): jnp.dot(cov_rows, a_panel, precision=highest, preferred_element_type=jnp....  58 us
    reduce_scatter x1, waiting for transfers between devices, per_device(): lax.psum_scatter(jnp.dot(cov_rows, a_panel, precision=highest, preferred_...  43.7 us
    reduce_scatter x1, waiting for transfers between devices, per_device(): lax.psum_scatter(jnp.dot(cov_rows, panel_flat, precision=highest, preferr...  43 us
    all_gather x1, waiting for transfers between devices, per_device(): full_b = lax.all_gather(factor_b, ('row', 'col'), axis=1, tiled=True)  38.1 us
  transfers between devices with their start and end apart: 8, of which 8 were waited for; matrix products, arithmetic and copies ran while one was open for 1% of the time, Pallas kernels for 0%

profile of v1, /device:TPU:0, one launch (start us, length us, event | category | flops | bytes accessed | tf_op | source)
XLA Modules:
  0.0 706.3 jit_solution(7979852990483669304)
XLA Ops:
  7.2 0.0 copy-start.4
  7.2 0.0 all-gather.3.cloned.1.call-start
  7.2 0.7 all-gather.3.cloned.1.call-update
  7.9 0.0 all-gather.5.cloned.1.call-start
  8.0 4.7 copy.27
  12.7 0.0 copy-start.1
  12.7 38.1 %all-gather.3.cloned.1.call-done = bf16[2,256,1024]{2,1,0:T(8,128)(2,1)} async-done(((bf16[2,16,1024]{2,1,0:T(8,128)(2,1)}), bf16[2,256,1024]{2,1,0:T(8,128)(2,1)}) %all-gather.3.cloned.1.call-update) | async-done | bytes 1048592 | tf_op jit(solution)/shard_map/all_gather | solution.py:30
  50.8 0.0 copy-done.4
  50.8 4.2 fusion.8
  55.0 0.0 all-gather.5.cloned.1.call-update
  55.0 0.0 copy-done.1
  55.0 0.0 reduce-scatter.3.cloned.1.call-start
  55.1 79.8 %all-gather.5.cloned.1.call-done = f32[2048,2,256]{2,0,1:T(8,128)} async-done(((f32[512,2,256]{2,0,1:T(8,128)}), f32[2048,2,256]{2,0,1:T(8,128)}) %all-gather.5.cloned.1.call-update) | async-done | bytes 4194320 | tf_op jit(solution)/shard_map/all_gather | solution.py:36
  134.9 5.4 copy.30
  140.3 32.4 %convolution_bitcast_fusion = f32[2048,512]{0,1:T(8,128)} fusion(f32[2048,512]{0,1:T(8,128)} %bitcast.38, f32[2048,2048]{1,0:T(8,128)} %param.4), kind=kOutput, calls=%fused_computation.7 | convolution fusion | flops 25769803776 | bytes 25165824 | tf_op jit(solution)/shard_map/dot_general | solution.py:45
  172.6 0.0 reduce-scatter.3.cloned.1.call-update
  172.7 0.0 reduce-scatter.5.cloned.1.call-start
  172.7 43.0 %reduce-scatter.3.cloned.1.call-done = f32[512,512]{0,1:T(8,128)} async-done(((f32[2048,512]{0,1:T(8,128)}), f32[512,512]{0,1:T(8,128)}) %reduce-scatter.3.cloned.1.call-update) | async-done | bytes 1048592 | tf_op jit(solution)/shard_map/reduce_scatter | solution.py:44
  215.7 1.6 copy.31
  217.3 1.2 all_to_all.32
  218.6 29.4 %all_to_all.40 = f32[16,1,16384]{2,1,0:T(1,128)S(1)} all-to-all(f32[16,1,16384]{2,1,0:T(1,128)S(1)} %all_to_all.32), channel_id=1, replica_groups=mesh['layer'=2,'row'=4,'col'=4] {'row','col'}, dimensions={0} | all-to-all | bytes 2097152 | tf_op jit(solution)/shard_map/all_to_all | solution.py:20
  247.9 2.5 reduce
  250.4 0.3 reshape.39
  250.8 0.7 copy.33
  251.4 1.4 all_to_all.33
  252.9 29.5 %all_to_all.41 = f32[16,1,16384]{2,1,0:T(1,128)S(1)} all-to-all(f32[16,1,16384]{2,1,0:T(1,128)S(1)} %all_to_all.33), channel_id=1, replica_groups=mesh['layer'=2,'row'=4,'col'=4] {'row','col'}, dimensions={0} | all-to-all | bytes 2097152 | tf_op jit(solution)/shard_map/all_to_all | solution.py:21
  282.4 3.0 multiply_reduce_fusion
  285.4 0.9 mul.26
  286.3 0.1 convert_add_fusion
  286.4 0.0 copy-start
  286.4 0.1 copy.48
  286.5 2.3 collective-permute-start
  288.8 23.7 %collective-permute-done = f32[512,512]{1,0:T(8,128)S(1)} collective-permute-done((f32[512,512]{1,0:T(8,128)S(1)}, f32[512,512]{1,0:T(8,128)S(1)}, u32[]{:S(2)}, u32[]{:S(2)}) %collective-permute-start) | collective-permute-done | bytes 1048608 | tf_op jit(solution)/shard_map/ppermute | solution.py:60
  312.5 1.5 pad_maximum_fusion
  314.0 1.7 collective-permute-start.1
  315.7 0.1 constant_dynamic-update-slice_fusion.5
  315.8 0.1 constant_dynamic-update-slice_fusion.4
  315.8 92.0 %collective-permute-done.1 = f32[1024,512]{1,0:T(8,128)} collective-permute-done((f32[1024,512]{1,0:T(8,128)}, f32[1024,512]{1,0:T(8,128)}, u32[]{:S(2)}, u32[]{:S(2)}) %collective-permute-start.1) | collective-permute-done | bytes 2097184 | tf_op jit(solution)/shard_map/ppermute | solution.py:60
  407.8 1.8 constant_dynamic-update-slice_fusion.3
  409.6 0.1 constant_dynamic-update-slice_fusion.2
  409.7 0.1 constant_dynamic-update-slice_fusion.1
  409.8 1.8 constant_dynamic-update-slice_fusion
  411.5 58.0 %fusion.4 = f32[2048,512]{0,1:T(8,128)} fusion(f32[2048,2048]{1,0:T(8,128)} %param.4, f32[4096,512]{1,0:T(8,128)S(1)} %constant_dynamic-update-slice_fusion, s32[]{:T(128)S(6)} %select_n.17), kind=kOutput, calls=%fused_computation.6 | convolution fusion | flops 25769803776 | bytes 25165828 | tf_op jit(solution)/shard_map/dot_general | solution.py:66
  469.5 0.0 reduce-scatter.5.cloned.1.call-update
  469.5 43.7 %reduce-scatter.5.cloned.1.call-done = f32[512,512]{0,1:T(8,128)} async-done(((f32[2048,512]{0,1:T(8,128)}), f32[512,512]{0,1:T(8,128)}) %reduce-scatter.5.cloned.1.call-update) | async-done | bytes 1048592 | tf_op jit(solution)/shard_map/reduce_scatter | solution.py:65
  513.2 1.6 copy.35
  514.8 1.2 all_to_all.34
  516.0 29.2 %all_to_all.42 = f32[16,1,16384]{2,1,0:T(1,128)S(1)} all-to-all(f32[16,1,16384]{2,1,0:T(1,128)S(1)} %all_to_all.34), channel_id=1, replica_groups=mesh['layer'=2,'row'=4,'col'=4] {'row','col'}, dimensions={0} | all-to-all | bytes 2097152 | tf_op jit(solution)/shard_map/all_to_all | solution.py:20
  545.3 3.8 reduce.2
  549.0 2.6 reshape.41
  551.7 2.9 copy.57
  554.6 3.3 all_to_all.35
  557.9 5.1 all-to-all-start.3
  563.0 0.2 all-reduce.2.cloned.1.call-start
  563.3 4.5 fusion.1
  567.8 18.2 %all-to-all-done.3 = f32[16,1,16384]{2,1,0:T(1,128)} async-done(((f32[16,1,16384]{2,1,0:T(1,128)}), f32[16,1,16384]{2,1,0:T(1,128)}, u32[]{:S(2)}, u32[]{:S(2)}) %all-to-all-start.3) | async-done | bytes 1048608 | tf_op jit(solution)/shard_map/all_to_all | solution.py:21
  586.0 4.7 reduce.3
  590.7 2.1 reshape_reshape.4
  592.8 0.0 copy-start.5
  592.8 4.8 fusion.9
  597.6 0.0 all-reduce.2.cloned.1.call-update
  597.6 100.3 %all-reduce.2.cloned.1.call-done = f32[2,256,1024]{2,1,0:T(8,128)} async-done(((f32[2,256,1024]{2,1,0:T(8,128)}), f32[2,256,1024]{2,1,0:T(8,128)}) %all-reduce.2.cloned.1.call-update) | async-done | bytes 2097168 | tf_op jit(solution)/shard_map/psum | solution.py:78
  698.0 0.0 copy-done.5
  698.0 1.6 multiply_add_fusion
  (5 shorter events, 0.0 us)
Async XLA Ops:
  7.2 43.6 %copy-start.4 = (bf16[512,2,256]{2,1,0:T(2,128)(2,1)S(1)}, bf16[512,2,256]{2,1,0:T(2,128)(2,1)}, u32[]{:S(2)}) copy-start(bf16[512,2,256]{2,1,0:T(2,128)(2,1)} %param.6) | copy-start | bytes 1572868
  7.2 43.6 %all-gather.3.cloned.1.call-start = ((), (), s32[]{:S(2)}) async-start(), calls=%async_computation.6 | async-start | bytes 1114112 | tf_op jit(solution)/shard_map/all_gather | solution.py:30
  7.9 127.0 %all-gather.5.cloned.1.call-start = ((), (), s32[]{:S(2)}) async-start(), calls=%async_computation.7 | async-start | bytes 5242880 | tf_op jit(solution)/shard_map/all_gather | solution.py:36
  12.7 42.3 %copy-start.1 = (bf16[512,2,1024]{0,2,1:T(8,128)(2,1)}, bf16[512,2,1024]{0,2,1:T(8,128)(2,1)S(1)}, u32[]{:S(2)}) copy-start(bf16[512,2,1024]{0,2,1:T(8,128)(2,1)S(1)} %copy.27) | copy-start | bytes 6291460
  55.0 160.7 %reduce-scatter.3.cloned.1.call-start = ((), (), s32[]{:S(2)}) async-start(), calls=%async_computation.8 | async-start | bytes 5242880 | tf_op jit(solution)/shard_map/reduce_scatter | solution.py:44
  172.7 340.6 %reduce-scatter.5.cloned.1.call-start = ((), (), s32[]{:S(2)}) async-start(), calls=%async_computation.9 | async-start | bytes 5242880 | tf_op jit(solution)/shard_map/reduce_scatter | solution.py:65
  286.4 276.9 %copy-start = (f32[128,8,256]{2,1,0:T(8,128)}, f32[128,8,256]{2,1,0:T(8,128)S(1)}, u32[]{:S(2)}) copy-start(f32[128,8,256]{2,1,0:T(8,128)S(1)} %convert_add_fusion) | copy-start | bytes 3145732
  286.5 26.1 %collective-permute-start = (f32[512,512]{1,0:T(8,128)S(1)}, f32[512,512]{1,0:T(8,128)S(1)}, u32[]{:S(2)}, u32[]{:S(2)}) collective-permute-start(f32[512,512]{1,0:T(8,128)S(1)} %bitcast.31), channel_id=1, source_target_pairs={{0,12},{4,0},{8,4},{12,8},{1,13},{5,1},{9,5},{13,9},{2,14},{6,2},{... | collective-permute-start | bytes 3145736 | tf_op jit(solution)/shard_map/ppermute | solution.py:60
  314.0 93.8 %collective-permute-start.1 = (f32[1024,512]{1,0:T(8,128)}, f32[1024,512]{1,0:T(8,128)}, u32[]{:S(2)}, u32[]{:S(2)}) collective-permute-start(f32[1024,512]{1,0:T(8,128)} %pad_maximum_fusion), channel_id=1, source_target_pairs={{0,8},{4,12},{8,0},{12,4},{1,9},{5,13},{9,1},{13,5},{2,10},{6,14},... | collective-permute-start | bytes 6291464 | tf_op jit(solution)/shard_map/ppermute | solution.py:60
  549.0 14.2 %copy-start.2 = (bf16[512,2,1024]{0,2,1:T(8,128)(2,1)S(1)}, bf16[512,2,1024]{0,2,1:T(8,128)(2,1)}, u32[]{:S(2)}) copy-start(bf16[512,2,1024]{0,2,1:T(8,128)(2,1)} %copy-done.1) | copy-start | bytes 6291460
  557.9 28.0 %all-to-all-start.3 = ((f32[16,1,16384]{2,1,0:T(1,128)}), f32[16,1,16384]{2,1,0:T(1,128)}, u32[]{:S(2)}, u32[]{:S(2)}) async-start(f32[16,1,16384]{2,1,0:T(1,128)} %all_to_all.35), calls=%async_computation.5 | async-start | bytes 2097152 | tf_op jit(solution)/shard_map/all_to_all | solution.py:21
  563.0 135.0 %all-reduce.2.cloned.1.call-start = ((), (), s32[]{:S(2)}) async-start(), calls=%async_computation.10 | async-start | bytes 4194304 | tf_op jit(solution)/shard_map/psum | solution.py:78
  567.8 25.0 %copy-start.3 = (bf16[512,2,1024]{0,2,1:T(8,128)(2,1)S(1)}, bf16[512,2,1024]{0,2,1:T(8,128)(2,1)}, u32[]{:S(2)}) copy-start(bf16[512,2,1024]{0,2,1:T(8,128)(2,1)} %fusion.1) | copy-start | bytes 6291460
  592.8 105.2 %copy-start.5 = (bf16[2,16,1024]{2,1,0:T(8,128)(2,1)S(1)}, bf16[2,16,1024]{2,1,0:T(8,128)(2,1)}, u32[]{:S(2)}) copy-start(bf16[2,16,1024]{2,1,0:T(8,128)(2,1)} %param.7) | copy-start | bytes 196612
Sparse Core Ops, SparseCore 0:
  10.2 40.5 all-gather.2
  55.1 79.7 all-gather.4
  172.8 42.9 reduce-scatter.2
  469.7 43.5 reduce-scatter.4
  597.8 100.1 all-reduce.1
